TPU v7x, 32 devices: a whole 2x2x4 slice. The times are simulated.
32 devices in a mesh: blk: 8 (over z, y), line: 4 (over x, core).
Axes of the slice: x: 2, y: 2, z: 4, core: 2. Of those that a mesh axis runs over, the one named last changes fastest.
Arguments:
- density: float32 [8, 64, 4096], P('blk', 'line'), may hold values from 0.5 to 1.5
- momentum: float32 [8, 3, 64, 4096], P('blk', None, 'line'), may hold values from -0.5 to 0.5
- energy: float32 [8, 64, 4096], P('blk', 'line'), may hold values from 2 to 4
- adjoint: float32 [8, 5, 64, 4096], P('blk', None, 'line'), may hold values from -6 to 6
- partners: int32 [8, 4], P('blk'), may hold values from 0 to 7
- counts: int32 [8], P('blk'), may hold values from 1 to 4, as said below
- orient: int32 [8, 4], P('blk'), may hold values from 0 to 1
Outputs:
- residual: float32 [8, 5, 64, 4096], P('blk', None, 'line')
- correction: float32 [8], P('blk')
Inputs may be any that keep to these rules, and one draw needn't show every extreme that they name: `partners`: slots at or past counts[b] are padding and are not read. `counts`: some block lists 4 partners.
All inputs are finite; a program needn't handle non-finite values.
Results may differ from a plain program's by a relative error of at most 0.0003.
Values sent between devices are 32-bit elements; how exact they have to be, the bound alone decides.
No kernel may reach another device: no remote copies, remote signals or barrier semaphores. Data moves between devices by JAX's collectives and lax.ppermute only.
A program may use at most 64 MiB of HBM per device.

v0:
```python
import jax
import jax.numpy as jnp
from jax import lax
from jax.sharding import PartitionSpec as P

stencil_one = 0.75
stencil_two = -0.15
stencil_three = 1.0 / 60.0
gamma_less = 0.4
viscosity = 0.5
conduction = 1.5
penalty = 4.0


def difference(fields, direction, start_row, extent):
    length = fields.shape[direction]

    def shifted(offset):
        return lax.slice_in_dim(fields, 3 + offset, length - 3 + offset, axis=direction)

    shape_list = [1] * fields.ndim
    shape_list[direction] = length - 6
    global_row = (start_row + 3 + jnp.arange(length - 6, dtype=jnp.int32)).reshape(shape_list)
    central_one = shifted(1) - shifted(-1)
    central_two = shifted(2) - shifted(-2)
    central_three = shifted(3) - shifted(-3)
    interior = stencil_one * central_one + stencil_two * central_two + stencil_three * central_three
    fourth = 2.0 / 3.0 * central_one - 1.0 / 12.0 * central_two
    second = 0.5 * central_one
    forward = shifted(1) - shifted(0)
    backward = shifted(0) - shifted(-1)
    result = jnp.where((global_row == 2) | (global_row == extent - 3), fourth, interior)
    result = jnp.where((global_row == 1) | (global_row == extent - 2), second, result)
    result = jnp.where(global_row == 0, forward, result)
    result = jnp.where(global_row == extent - 1, backward, result)
    return result


def primitives(fields):
    density_raw = fields[:, 0:1]
    density_safe = jnp.where(density_raw == 0.0, 1.0, density_raw)
    velocity = fields[:, 1:4] / density_safe
    kinetic = 0.5 * jnp.sum(fields[:, 1:4] * velocity, axis=1, keepdims=True)
    pressure = gamma_less * (fields[:, 4:5] - kinetic)
    return (velocity, pressure, density_safe)


def direction_residual(fields, direction, start_row, extent, normal_index):
    velocity, pressure, density_safe = primitives(fields)
    primitive = jnp.concatenate([velocity, pressure / density_safe], axis=1)
    gradient = difference(primitive, direction, start_row, extent)
    length = fields.shape[direction]
    middle = lax.slice_in_dim(fields, 3, length - 3, axis=direction)
    mid_velocity = lax.slice_in_dim(velocity, 3, length - 3, axis=direction)
    mid_pressure = lax.slice_in_dim(pressure, 3, length - 3, axis=direction)
    normal_speed = mid_velocity[:, normal_index : normal_index + 1]
    selector = (jnp.arange(3) == normal_index).astype(fields.dtype).reshape(1, 3, 1, 1)
    convective = jnp.concatenate(
        [
            middle[:, normal_index + 1 : normal_index + 2],
            middle[:, 1:4] * normal_speed + mid_pressure * selector,
            (middle[:, 4:5] + mid_pressure) * normal_speed,
        ],
        axis=1,
    )
    viscous = jnp.concatenate(
        [
            jnp.zeros_like(normal_speed),
            viscosity * gradient[:, 0:3],
            viscosity * conduction * gradient[:, 3:4],
        ],
        axis=1,
    )
    return difference(convective - viscous, direction, start_row + 3, extent)


def per_device(density, momentum, energy, adjoint, partners, counts, orient):
    state = jnp.concatenate([density[:, None], momentum, energy[:, None]], axis=1)
    xrows = state.shape[2]
    yextent = state.shape[3]
    line_count = lax.axis_size("line")
    block_count = lax.axis_size("blk")
    xextent = xrows * line_count
    lines = lax.all_to_all(state, "line", split_axis=3, concat_axis=2, tiled=True)
    padded_lines = jnp.pad(lines, ((0, 0), (0, 0), (6, 6), (0, 0)))
    line_part = direction_residual(padded_lines, 2, -6, xextent, 0)
    xpart = lax.all_to_all(line_part, "line", split_axis=2, concat_axis=3, tiled=True)
    padded_y = jnp.pad(state, ((0, 0), (0, 0), (0, 0), (6, 6)))
    ypart = direction_residual(padded_y, 3, -6, yextent, 1)
    result = xpart + ypart
    bottom_row = state[:, :, :, 0]
    gathered = lax.all_gather(bottom_row, "blk", axis=0, tiled=True)
    slots = jnp.arange(partners.shape[1], dtype=jnp.int32)
    listed = partners[0]
    count_here = counts[0]
    weights = jnp.where(slots < count_here, 1.0 / count_here.astype(jnp.float32), jnp.float32(0.0))
    onehot = (listed[:, None] == jnp.arange(block_count, dtype=jnp.int32)[None, :]).astype(
        jnp.float32
    ) * weights[:, None]
    picked = jnp.einsum("kb,bvx->kvx", onehot, gathered, precision=lax.Precision.HIGHEST)
    signs = (
        jnp.ones((partners.shape[1], 5), jnp.float32)
        .at[:, 2]
        .set(1.0 - 2.0 * orient[0].astype(jnp.float32))
    )
    target = jnp.sum(picked * signs[:, :, None], axis=0)[None]
    result = result.at[:, :, :, yextent - 1].add(penalty * (state[:, :, :, yextent - 1] - target))
    total = lax.psum(jnp.sum(adjoint * result), "line")
    correction = (total / (xextent * yextent)).reshape(1)
    return (result, correction)


def solution(mesh):
    return jax.shard_map(
        per_device,
        mesh=mesh,
        in_specs=(
            P("blk", "line", None),
            P("blk", None, "line", None),
            P("blk", "line", None),
            P("blk", None, "line", None),
            P("blk", None),
            P("blk"),
            P("blk", None),
        ),
        out_specs=(P("blk", None, "line", None), P("blk")),
        check_vma=False,
    )
```

profile of v0, /device:TPU:0, one launch (start us, length us, event | category | flops | bytes accessed | tf_op | source)
XLA Modules:
  0.0 212.0 jit_solution(9206048323847633590)
XLA Ops:
  0.6 1.4 pad_maximum_fusion
  2.0 14.9 %copy.63 = f32[1,5,16,4096]{2,0,1,3:T(1,128)} copy(f32[1,5,16,4096]{3,2,1,0:T(8,128)S(1)} %pad_maximum_fusion) | data formatting | bytes 2621440 | tf_op jit(solution)/shard_map/concatenate | solution.py:78
  17.4 34.3 %reduce.12 = f32[4096,5,16]{2,1,0:T(8,128)} reduce(f32[4096,5,1,16]{3,2,1,0:T(1,128)} %bitcast.52, f32[]{:T(128)} %broadcast.383), dimensions={2}, to_apply=%bitcast.41.reduce_sub_computation | reduce | bytes 2621444
  51.7 9.3 %reshape.473 = f32[4,1,81920]{2,1,0:T(1,128)} reshape(f32[4096,5,16]{2,1,0:T(8,128)} %reduce.12) | data formatting | bytes 2621440
  61.0 4.2 %all-to-all-start = ((f32[4,1,81920]{2,1,0:T(1,128)}), f32[4,1,81920]{2,1,0:T(1,128)S(1)}, u32[]{:S(2)}, u32[]{:S(2)}) async-start(f32[4,1,81920]{2,1,0:T(1,128)} %reshape.473), calls=%async_computation | async-start | bytes 2621440 | tf_op jit(solution)/shard_map/all_to_all | solution.py:84
  65.3 0.6 compare_or_fusion.2
  66.7 0.7 compare_reduce_fusion
  68.1 1.3 pad_slice_fusion.35
  69.4 1.7 fusion.35
  71.2 1.0 copy-done.3
  72.2 0.7 slice-done
  73.0 31.8 %all-gather = f32[8,5,16,1]{2,3,1,0:T(1,128)S(1)} all-gather(f32[1,5,16,1]{2,3,1,0:T(1,128)S(1)} %copy.75), channel_id=2, replica_groups=mesh['blk'=8,'line'=4] {'blk'}, dimensions={0}, use_global_device_ids=true | all-gather | bytes 2880 | tf_op jit(solution)/shard_map/all_gather | solution.py:92
  105.4 0.6 fusion.79
  106.5 2.2 %fusion.46 = f32[1,3,16,4102]{3,2,1,0:T(8,128)} fusion(f32[1,5,16,4096]{3,2,1,0:T(8,128)S(1)} %copy-done.1, f32[3]{0:T(128)S(1)} %compare_convert_fusion, f32[16,4102]{1,0:T(8,128)} %get-tuple-element.45, f32[16,4102]{1,0:T(8,128)} %get-tuple-element.43), kind=kLoop, calls=%fused_computation.96 | loop fusion | flops 590688 | bytes 2623372 | tf_op jit(solution)/shard_map/add | solution.py:61
  108.7 1.7 slice_multiply_fusion.3
  110.4 5.5 %reduce.13 = f32[4,81920]{1,0:T(4,128)} reduce(f32[4,1,81920]{2,1,0:T(1,128)S(1)} %all-to-all-done, f32[]{:T(128)} %broadcast.383), dimensions={1}, to_apply=%all_to_all.26.reduce_sub_computation | reduce | bytes 2621444 | tf_op jit(solution)/shard_map/all_to_all | solution.py:84
  115.9 27.3 %reshape.474 = f32[4096,5,1,16]{3,2,1,0:T(1,128)} reshape(f32[4,81920]{1,0:T(4,128)} %reduce.13) | data formatting | bytes 2621440
  143.1 19.8 %copy.64 = f32[1,5,16,4096]{3,2,1,0:T(8,128)} copy(f32[1,5,16,4096]{2,0,1,3:T(1,128)} %bitcast.53) | data formatting | bytes 2621440 | tf_op jit(solution)/shard_map/all_to_all | solution.py:84
  162.9 2.2 %all_to_all.27 = f32[1,5,16,4,1024]{4,3,2,1,0:T(4,128)S(1)} reshape(f32[1,5,16,4096]{3,2,1,0:T(8,128)} %copy.64) | data formatting | bytes 2621440 | tf_op jit(solution)/shard_map/all_to_all | solution.py:84
  165.1 0.7 copy.65
  166.8 1.5 fusion.20
  169.1 1.4 fusion.12
  170.5 2.4 %copy.66 = f32[1,5,64,1024]{3,0,1,2:T(1,128)} copy(f32[1,5,64,1024]{3,2,1,0:T(8,128)S(1)} %fusion.12) | data formatting | bytes 2621440 | tf_op jit(solution)/shard_map/jit(_where)/select_n | solution.py:35
  172.9 4.3 %all-to-all-start.1 = ((f32[1,5,64,1024]{3,0,1,2:T(1,128)}), f32[1,5,64,1024]{3,0,1,2:T(1,128)}, u32[]{:S(2)}, u32[]{:S(2)}) async-start(f32[1,5,64,1024]{3,0,1,2:T(1,128)} %copy.66), calls=%async_computation.1 | async-start | bytes 2621440 | tf_op jit(solution)/shard_map/all_to_all | solution.py:87
  177.2 1.6 maximum_subtract_fusion.1
  178.7 15.7 %all-to-all-done.1 = f32[1,5,64,1024]{3,0,1,2:T(1,128)} async-done(((f32[1,5,64,1024]{3,0,1,2:T(1,128)}), f32[1,5,64,1024]{3,0,1,2:T(1,128)}, u32[]{:S(2)}, u32[]{:S(2)}) %all-to-all-start.1) | async-done | bytes 1310752 | tf_op jit(solution)/shard_map/all_to_all | solution.py:87
  194.5 1.6 copy.67
  196.2 2.1 fusion.6
  198.3 1.0 copy-done.2
  199.4 1.8 scatter-add.4
  201.2 2.7 %multiply_reduce_fusion = f32[]{:T(128)} fusion(f32[1,5,16,4096]{3,2,1,0:T(8,128)} %param.14, f32[1,5,16,4096]{3,2,1,0:T(8,128)} %scatter-add.4), kind=kLoop, calls=%fused_computation.50 | loop fusion | flops 655359 | bytes 2621444 | tf_op jit(solution)/shard_map/reduce_sum | solution.py:108
  203.9 6.4 %psum.7 = f32[]{:T(128)} all-reduce(f32[]{:T(128)} %multiply_reduce_fusion), channel_id=1, replica_groups=mesh['blk'=8,'line'=4] {'line'}, use_global_device_ids=true, to_apply=%region_5.6 | all-reduce | flops 1 | bytes 8 | tf_op jit(solution)/shard_map/psum | solution.py:108
  (48 shorter events, 4.4 us)
Async XLA Ops:
  2.0 66.1 %copy-start = (f32[1,5,16,4096]{3,2,1,0:T(8,128)}, f32[1,5,16,4096]{3,2,1,0:T(8,128)S(1)}, u32[]{:S(2)}) copy-start(f32[1,5,16,4096]{3,2,1,0:T(8,128)S(1)} %pad_maximum_fusion) | copy-start | bytes 3932164
  61.0 49.3 %all-to-all-start = ((f32[4,1,81920]{2,1,0:T(1,128)}), f32[4,1,81920]{2,1,0:T(1,128)S(1)}, u32[]{:S(2)}, u32[]{:S(2)}) async-start(f32[4,1,81920]{2,1,0:T(1,128)} %reshape.473), calls=%async_computation | async-start | bytes 2621440 | tf_op jit(solution)/shard_map/all_to_all | solution.py:84
  71.2 1.0 copy-start.3
  72.1 0.8 slice-start
  72.1 33.3 %copy-start.7 = (s32[1,4]{1,0:T(1,128)S(1)}, s32[1,4]{1,0:T(1,128)}, u32[]{:S(2)}) copy-start(s32[1,4]{1,0:T(1,128)} %param.17) | copy-start | bytes 52
  72.1 34.0 %copy-start.8 = (s32[1,4]{1,0:T(1,128)S(1)}, s32[1,4]{1,0:T(1,128)}, u32[]{:S(2)}) copy-start(s32[1,4]{1,0:T(1,128)} %param.15) | copy-start | bytes 52
  72.1 34.3 %copy-start.1 = (f32[1,5,16,4096]{3,2,1,0:T(8,128)S(1)}, f32[1,5,16,4096]{3,2,1,0:T(8,128)}, u32[]{:S(2)}) copy-start(f32[1,5,16,4096]{3,2,1,0:T(8,128)} %copy-done) | copy-start | bytes 3932164
  166.2 0.7 copy-start.4
  166.2 0.7 copy-start.5
  166.2 0.7 copy-start.6
  172.9 21.6 %all-to-all-start.1 = ((f32[1,5,64,1024]{3,0,1,2:T(1,128)}), f32[1,5,64,1024]{3,0,1,2:T(1,128)}, u32[]{:S(2)}, u32[]{:S(2)}) async-start(f32[1,5,64,1024]{3,0,1,2:T(1,128)} %copy.66), calls=%async_computation.1 | async-start | bytes 2621440 | tf_op jit(solution)/shard_map/all_to_all | solution.py:87
  198.3 1.1 copy-start.2
where the time goes:
time: 213 us; the launch traced here: 212 us
  local copies, waits for them, and re-layouts  84.1 us (39%)
  other arithmetic  61.9 us (29%)
  blocking collectives  38.1 us (18%)
  waiting for transfers between devices  15.7 us (7%)
  starting transfers between devices  8.53 us (4%)
  between operations  3.44 us (2%)
    unnamed x22, local copies, waits for them, and re-layouts  39.8 us
    unnamed x1, other arithmetic  34.3 us
    all_gather x1, blocking collectives, per_device(): gathered = lax.all_gather(bottom_row, 'blk', axis=0, tiled=True)  31.8 us
    all_to_all x3, local copies, waits for them, and re-layouts, per_device(): lax.all_to_all(state, 'line', split_axis=3, concat_axis=2, tiled=True)  22.7 us
    all_to_all x1, waiting for transfers between devices, per_device(): lax.all_to_all(line_part, 'line', split_axis=2, concat_axis=3, tiled=True)  15.7 us
    concatenate x1, local copies, waits for them, and re-layouts, per_device(): jnp.concatenate([density[:, None], momentum, energy[:, None]], axis=1)  14.9 us
    psum x1, blocking collectives, per_device(): total = lax.psum(jnp.sum(adjoint * result), 'line')  6.37 us
    all_to_all x1, other arithmetic, per_device(): lax.all_to_all(state, 'line', split_axis=3, concat_axis=2, tiled=True)  5.48 us
  transfers between devices with their start and end apart: 2, of which 1 were waited for; matrix products, arithmetic and copies ran while one was open for 6% of the time, Pallas kernels for 0%

commit v1 on v0

--- a/solution.py
+++ b/solution.py
@@ -10,6 +10,12 @@
 viscosity = 0.5
 conduction = 1.5
 penalty = 4.0
+
+
+def in_order(parts, dim):
+    parts = jnp.moveaxis(parts, 0, dim)
+    shape = parts.shape
+    return parts.reshape(*shape[:dim], shape[dim] * shape[dim + 1], *shape[dim + 2 :])
 
 
 def difference(fields, direction, start_row, extent):
@@ -89,7 +95,14 @@
     ypart = direction_residual(padded_y, 3, -6, yextent, 1)
     result = xpart + ypart
     bottom_row = state[:, :, :, 0]
-    gathered = lax.all_gather(bottom_row, "blk", axis=0, tiled=True)
+    peers = lax.axis_size("blk")
+    forward_2 = [(i, (i + 1) % peers) for i in range(peers)]
+    parts = [bottom_row]
+    while len(parts) < peers:
+        parts.append(lax.ppermute(parts[-1], "blk", forward_2))
+    position = lax.axis_index("blk")
+    parts = jnp.stack(parts)[(position - jnp.arange(peers)) % peers]
+    gathered = in_order(parts, 0)
     slots = jnp.arange(partners.shape[1], dtype=jnp.int32)
     listed = partners[0]
     count_here = counts[0]

time: 213 us -> 204 us (0.958)
  blocking collectives: 38.1 us -> 6.37 us
  waiting for transfers between devices: 15.7 us -> 33.3 us
  starting transfers between devices: 8.53 us -> 13.7 us
  other arithmetic: 61.9 us -> 59.7 us
    all_gather x1 -> x0, blocking collectives: 31.8 us -> none  [per_device(): gathered = lax.all_gather(bottom_row, 'blk', axis=0, tiled=True)]
    ppermute x0 -> x7, waiting for transfers between devices: none -> 29.9 us  [per_device(): parts.append(lax.ppermute(parts[-1], 'blk', forward_2))]
    all_to_all x1, waiting for transfers between devices: 15.7 us -> 3.45 us  [per_device(): lax.all_to_all(line_part, 'line', split_axis=2, concat_axis=3, tiled=True)]
    ppermute x0 -> x7, starting transfers between devices: none -> 4.69 us  [per_device(): parts.append(lax.ppermute(parts[-1], 'blk', forward_2))]
    all_to_all x3, local copies, waits for them, and re-layouts: 22.7 us -> 24.9 us  [per_device(): lax.all_to_all(state, 'line', split_axis=3, concat_axis=2, tiled=True)]
    unnamed x22 -> x28, local copies, waits for them, and re-layouts: 39.8 us -> 39.9 us
  transfers between devices with their start and end apart: 2 -> 9, of which waited for: 1 -> 6; matrix products, arithmetic and copies ran while one was open for 6% -> 35% of each run, Pallas kernels for 0% -> 0%
where the time goes in v1:
time: 204 us; the launch traced here: 203 us
  local copies, waits for them, and re-layouts  86.1 us (42%)
  other arithmetic  59.7 us (29%)
  waiting for transfers between devices  33.3 us (16%)
  starting transfers between devices  13.7 us (7%)
  blocking collectives  6.37 us (3%)
  between operations  3.49 us (2%)
    unnamed x28, local copies, waits for them, and re-layouts  39.9 us
    unnamed x1, other arithmetic  35.5 us
    ppermute x7, waiting for transfers between devices, per_device(): parts.append(lax.ppermute(parts[-1], 'blk', forward_2))  29.9 us
    all_to_all x3, local copies, waits for them, and re-layouts, per_device(): lax.all_to_all(state, 'line', split_axis=3, concat_axis=2, tiled=True)  24.9 us
    concatenate x1, local copies, waits for them, and re-layouts, per_device(): jnp.concatenate([density[:, None], momentum, energy[:, None]], axis=1)  14.7 us
    all_to_all x1, other arithmetic, per_device(): lax.all_to_all(state, 'line', split_axis=3, concat_axis=2, tiled=True)  6.44 us
    psum x1, blocking collectives, per_device(): total = lax.psum(jnp.sum(adjoint * result), 'line')  6.37 us
    ppermute x7, starting transfers between devices, per_device(): parts.append(lax.ppermute(parts[-1], 'blk', forward_2))  4.69 us
  transfers between devices with their start and end apart: 9, of which 6 were waited for; matrix products, arithmetic and copies ran while one was open for 35% of the time, Pallas kernels for 0%

profile of v1, /device:TPU:0, one launch (start us, length us, event | category | flops | bytes accessed | tf_op | source)
XLA Modules:
  0.0 202.9 jit_solution(4248050468235166495)
XLA Ops:
  0.6 1.4 pad_maximum_fusion
  2.0 14.7 %copy.61 = f32[1,5,16,4096]{2,0,1,3:T(1,128)} copy(f32[1,5,16,4096]{3,2,1,0:T(8,128)S(1)} %pad_maximum_fusion) | data formatting | bytes 2621440 | tf_op jit(solution)/shard_map/concatenate | solution.py:84
  17.3 35.5 %reduce.15 = f32[4096,5,16]{2,1,0:T(8,128)} reduce(f32[4096,5,1,16]{3,2,1,0:T(1,128)} %bitcast.83, f32[]{:T(128)} %broadcast.454), dimensions={2}, to_apply=%bitcast.71.reduce_sub_computation | reduce | bytes 2621444
  52.8 9.3 %reshape.538 = f32[4,1,81920]{2,1,0:T(1,128)} reshape(f32[4096,5,16]{2,1,0:T(8,128)} %reduce.15) | data formatting | bytes 2621440
  62.0 4.3 %all-to-all-start = ((f32[4,1,81920]{2,1,0:T(1,128)}), f32[4,1,81920]{2,1,0:T(1,128)}, u32[]{:S(2)}, u32[]{:S(2)}) async-start(f32[4,1,81920]{2,1,0:T(1,128)} %reshape.538), calls=%async_computation | async-start | bytes 2621440 | tf_op jit(solution)/shard_map/all_to_all | solution.py:90
  66.4 3.0 %collective-permute-start = (f32[1,5,16]{2,0,1:T(1,128)S(1)}, f32[1,5,16]{2,0,1:T(1,128)S(1)}, u32[]{:S(2)}, u32[]{:S(2)}) collective-permute-start(f32[1,5,16]{2,0,1:T(1,128)S(1)} %squeeze.9), channel_id=1, source_target_pairs={{0,4},{4,8},{8,12},{12,16},{16,20},{20,24},{24,28},{28,0},{1,5},{5... | collective-permute-start | bytes 968 | tf_op jit(solution)/shard_map/ppermute | solution.py:102
  71.5 1.7 fusion.35
  73.3 0.7 slice_multiply_fusion.3
  74.1 0.7 compare_reduce_fusion
  74.8 1.1 pad_slice_fusion.35
  79.2 1.6 collective-permute-start.1
  80.7 4.8 %collective-permute-done.1 = f32[1,5,16]{2,0,1:T(1,128)S(1)} collective-permute-done((f32[1,5,16]{2,0,1:T(1,128)S(1)}, f32[1,5,16]{2,0,1:T(1,128)S(1)}, u32[]{:S(2)}, u32[]{:S(2)}) %collective-permute-start.1) | collective-permute-done | bytes 352 | tf_op jit(solution)/shard_map/ppermute | solution.py:102
  85.5 6.3 %collective-permute-done.2 = f32[1,5,16]{2,0,1:T(1,128)S(1)} collective-permute-done((f32[1,5,16]{2,0,1:T(1,128)S(1)}, f32[1,5,16]{2,0,1:T(1,128)S(1)}, u32[]{:S(2)}, u32[]{:S(2)}) %collective-permute-start.2) | collective-permute-done | bytes 352 | tf_op jit(solution)/shard_map/ppermute | solution.py:102
  91.8 6.3 %collective-permute-done.3 = f32[1,5,16]{2,0,1:T(1,128)S(1)} collective-permute-done((f32[1,5,16]{2,0,1:T(1,128)S(1)}, f32[1,5,16]{2,0,1:T(1,128)S(1)}, u32[]{:S(2)}, u32[]{:S(2)}) %collective-permute-start.3) | collective-permute-done | bytes 352 | tf_op jit(solution)/shard_map/ppermute | solution.py:102
  98.1 6.4 %reduce.16 = f32[4,81920]{1,0:T(4,128)} reduce(f32[4,1,81920]{2,1,0:T(1,128)} %all-to-all-done, f32[]{:T(128)} %broadcast.454), dimensions={1}, to_apply=%all_to_all.26.reduce_sub_computation | reduce | bytes 2621444 | tf_op jit(solution)/shard_map/all_to_all | solution.py:90
  104.5 27.3 %reshape.539 = f32[4096,5,1,16]{3,2,1,0:T(1,128)} reshape(f32[4,81920]{1,0:T(4,128)} %reduce.16) | data formatting | bytes 2621440
  131.8 19.8 %copy.62 = f32[1,5,16,4096]{3,2,1,0:T(8,128)} copy(f32[1,5,16,4096]{2,0,1,3:T(1,128)} %bitcast.84) | data formatting | bytes 2621440 | tf_op jit(solution)/shard_map/all_to_all | solution.py:90
  151.6 3.0 %all_to_all.27 = f32[1,5,16,4,1024]{4,3,2,1,0:T(4,128)} reshape(f32[1,5,16,4096]{3,2,1,0:T(8,128)} %copy.62) | data formatting | bytes 2621440 | tf_op jit(solution)/shard_map/all_to_all | solution.py:90
  154.6 2.1 %copy.63 = f32[1,5,4,16,1024]{4,3,2,1,0:T(8,128)S(1)} copy(f32[1,5,4,16,1024]{4,2,3,1,0:T(4,128)} %bitcast.85) | data formatting | bytes 2621440 | tf_op jit(solution)/shard_map/all_to_all | solution.py:90
  157.7 1.4 fusion.20
  159.9 1.4 fusion.12
  161.3 2.4 %copy.64 = f32[1,5,64,1024]{3,0,1,2:T(1,128)} copy(f32[1,5,64,1024]{3,2,1,0:T(8,128)S(1)} %fusion.12) | data formatting | bytes 2621440 | tf_op jit(solution)/shard_map/jit(_where)/select_n | solution.py:41
  163.7 4.7 %all-to-all-start.1 = ((f32[1,5,64,1024]{3,0,1,2:T(1,128)}), f32[1,5,64,1024]{3,0,1,2:T(1,128)}, u32[]{:S(2)}, u32[]{:S(2)}) async-start(f32[1,5,64,1024]{3,0,1,2:T(1,128)} %copy.64), calls=%async_computation.1 | async-start | bytes 2621440 | tf_op jit(solution)/shard_map/all_to_all | solution.py:93
  168.5 6.3 %collective-permute-done.5 = f32[1,5,16]{2,0,1:T(1,128)S(1)} collective-permute-done((f32[1,5,16]{2,0,1:T(1,128)S(1)}, f32[1,5,16]{2,0,1:T(1,128)S(1)}, u32[]{:S(2)}, u32[]{:S(2)}) %collective-permute-start.5) | collective-permute-done | bytes 352 | tf_op jit(solution)/shard_map/ppermute | solution.py:102
  174.8 6.3 %collective-permute-done.6 = f32[1,5,16]{2,0,1:T(1,128)S(1)} collective-permute-done((f32[1,5,16]{2,0,1:T(1,128)S(1)}, f32[1,5,16]{2,0,1:T(1,128)S(1)}, u32[]{:S(2)}, u32[]{:S(2)}) %collective-permute-start.6) | collective-permute-done | bytes 352 | tf_op jit(solution)/shard_map/ppermute | solution.py:102
  182.0 3.4 %all-to-all-done.1 = f32[1,5,64,1024]{3,0,1,2:T(1,128)} async-done(((f32[1,5,64,1024]{3,0,1,2:T(1,128)}), f32[1,5,64,1024]{3,0,1,2:T(1,128)}, u32[]{:S(2)}, u32[]{:S(2)}) %all-to-all-start.1) | async-done | bytes 1310752 | tf_op jit(solution)/shard_map/all_to_all | solution.py:93
  185.4 1.6 copy.65
  187.1 2.1 %fusion.6 = f32[1,5,16,4096]{3,2,1,0:T(8,128)S(1)} fusion(f32[1,5,16,4096]{3,2,1,0:T(8,128)S(1)} %bitcast.87, f32[1,5,16,4102]{3,2,1,0:T(8,128)S(1)} %maximum_subtract_fusion.1, pred[4096]{0:T(1024)(128)(4,1)S(1)} %get-tuple-element.59, pred[4096]{0:T(1024)(128)(4,1)S(1)} %get-tuple-element.58, pred[4096]{0:T(1024)(128)(4,1)S(1)} %get-tuple-element.56, ...), kind=kLoop, calls=%fused_computation.40 | loop fusion | flops 6225920 | bytes 11812864 | tf_op jit(solution)/shard_map/add | solution.py:96
  189.2 1.0 copy-done
  190.4 1.8 scatter-add.4
  192.2 2.7 %multiply_reduce_fusion = f32[]{:T(128)} fusion(f32[1,5,16,4096]{3,2,1,0:T(8,128)} %param.14, f32[1,5,16,4096]{3,2,1,0:T(8,128)} %scatter-add.4), kind=kLoop, calls=%fused_computation.51 | loop fusion | flops 655359 | bytes 2621444 | tf_op jit(solution)/shard_map/reduce_sum | solution.py:121
  194.8 6.4 %psum.7 = f32[]{:T(128)} all-reduce(f32[]{:T(128)} %multiply_reduce_fusion), channel_id=1, replica_groups=mesh['blk'=8,'line'=4] {'line'}, use_global_device_ids=true, to_apply=%region_5.6 | all-reduce | flops 1 | bytes 8 | tf_op jit(solution)/shard_map/psum | solution.py:121
  (72 shorter events, 8.0 us)
Async XLA Ops:
  62.0 36.0 %all-to-all-start = ((f32[4,1,81920]{2,1,0:T(1,128)}), f32[4,1,81920]{2,1,0:T(1,128)}, u32[]{:S(2)}, u32[]{:S(2)}) async-start(f32[4,1,81920]{2,1,0:T(1,128)} %reshape.538), calls=%async_computation | async-start | bytes 2621440 | tf_op jit(solution)/shard_map/all_to_all | solution.py:90
  66.4 12.7 %collective-permute-start = (f32[1,5,16]{2,0,1:T(1,128)S(1)}, f32[1,5,16]{2,0,1:T(1,128)S(1)}, u32[]{:S(2)}, u32[]{:S(2)}) collective-permute-start(f32[1,5,16]{2,0,1:T(1,128)S(1)} %squeeze.9), channel_id=1, source_target_pairs={{0,4},{4,8},{8,12},{12,16},{16,20},{20,24},{24,28},{28,0},{1,5},{5... | collective-permute-start | bytes 968 | tf_op jit(solution)/shard_map/ppermute | solution.py:102
  76.7 1.0 copy-start.1
  76.7 1.0 copy-start.2
  76.7 1.1 copy-start.3
  77.8 0.7 copy-start.7
  79.2 6.3 %collective-permute-start.1 = (f32[1,5,16]{2,0,1:T(1,128)S(1)}, f32[1,5,16]{2,0,1:T(1,128)S(1)}, u32[]{:S(2)}, u32[]{:S(2)}) collective-permute-start(f32[1,5,16]{2,0,1:T(1,128)S(1)} %collective-permute-done), channel_id=1, source_target_pairs={{0,4},{4,8},{8,12},{12,16},{16,20},{20,24},{24,28},{28,0},{1,5},{5... | collective-permute-start | bytes 968 | tf_op jit(solution)/shard_map/ppermute | solution.py:102
  85.5 6.3 %collective-permute-start.2 = (f32[1,5,16]{2,0,1:T(1,128)S(1)}, f32[1,5,16]{2,0,1:T(1,128)S(1)}, u32[]{:S(2)}, u32[]{:S(2)}) collective-permute-start(f32[1,5,16]{2,0,1:T(1,128)S(1)} %collective-permute-done.1), channel_id=1, source_target_pairs={{0,4},{4,8},{8,12},{12,16},{16,20},{20,24},{24,28},{28,0},{1,5},{5... | collective-permute-start | bytes 968 | tf_op jit(solution)/shard_map/ppermute | solution.py:102
  91.8 6.3 %collective-permute-start.3 = (f32[1,5,16]{2,0,1:T(1,128)S(1)}, f32[1,5,16]{2,0,1:T(1,128)S(1)}, u32[]{:S(2)}, u32[]{:S(2)}) collective-permute-start(f32[1,5,16]{2,0,1:T(1,128)S(1)} %collective-permute-done.2), channel_id=1, source_target_pairs={{0,4},{4,8},{8,12},{12,16},{16,20},{20,24},{24,28},{28,0},{1,5},{5... | collective-permute-start | bytes 968 | tf_op jit(solution)/shard_map/ppermute | solution.py:102
  98.1 70.3 %collective-permute-start.4 = (f32[1,5,16]{2,0,1:T(1,128)S(1)}, f32[1,5,16]{2,0,1:T(1,128)S(1)}, u32[]{:S(2)}, u32[]{:S(2)}) collective-permute-start(f32[1,5,16]{2,0,1:T(1,128)S(1)} %collective-permute-done.3), channel_id=1, source_target_pairs={{0,4},{4,8},{8,12},{12,16},{16,20},{20,24},{24,28},{28,0},{1,5},{5... | collective-permute-start | bytes 968 | tf_op jit(solution)/shard_map/ppermute | solution.py:102
  157.0 0.7 copy-start.4
  157.0 0.7 copy-start.5
  157.0 0.7 copy-start.6
  163.7 17.9 %copy-start.8 = (s32[1,4]{1,0:T(1,128)S(1)}, s32[1,4]{1,0:T(1,128)}, u32[]{:S(2)}) copy-start(s32[1,4]{1,0:T(1,128)} %param.15) | copy-start | bytes 52
  163.7 21.7 %all-to-all-start.1 = ((f32[1,5,64,1024]{3,0,1,2:T(1,128)}), f32[1,5,64,1024]{3,0,1,2:T(1,128)}, u32[]{:S(2)}, u32[]{:S(2)}) async-start(f32[1,5,64,1024]{3,0,1,2:T(1,128)} %copy.64), calls=%async_computation.1 | async-start | bytes 2621440 | tf_op jit(solution)/shard_map/all_to_all | solution.py:93
  168.4 6.3 %collective-permute-start.5 = (f32[1,5,16]{2,0,1:T(1,128)S(1)}, f32[1,5,16]{2,0,1:T(1,128)S(1)}, u32[]{:S(2)}, u32[]{:S(2)}) collective-permute-start(f32[1,5,16]{2,0,1:T(1,128)S(1)} %collective-permute-done.4), channel_id=1, source_target_pairs={{0,4},{4,8},{8,12},{12,16},{16,20},{20,24},{24,28},{28,0},{1,5},{5... | collective-permute-start | bytes 968 | tf_op jit(solution)/shard_map/ppermute | solution.py:102
  174.8 6.3 %collective-permute-start.6 = (f32[1,5,16]{2,0,1:T(1,128)S(1)}, f32[1,5,16]{2,0,1:T(1,128)S(1)}, u32[]{:S(2)}, u32[]{:S(2)}) collective-permute-start(f32[1,5,16]{2,0,1:T(1,128)S(1)} %collective-permute-done.5), channel_id=1, source_target_pairs={{0,4},{4,8},{8,12},{12,16},{16,20},{20,24},{24,28},{28,0},{1,5},{5... | collective-permute-start | bytes 968 | tf_op jit(solution)/shard_map/ppermute | solution.py:102
  189.2 1.1 copy-start
